TPU v7x, 32 devices: a whole 2x2x4 slice. The times are simulated.
32 devices in a mesh: dp: 4 (over z), expert: 8 (over y, x, core).
Axes of the slice: x: 2, y: 2, z: 4, core: 2. Of those that a mesh axis runs over, the one named last changes fastest.
Arguments:
- tokens: bfloat16 [4096, 4096], P(('dp', 'expert')), may hold values from -6 to 6
- chosen: int32 [32, 128], replicated, may hold values from 0 to 4095, as said below
- gate_levels: int32 [32, 128], replicated, may hold values from 32 to 255
- expert_gate: bfloat16 [32, 4096, 768], P(('dp', 'expert')), may hold values from -0.09375 to 0.09375
- expert_up: bfloat16 [32, 4096, 768], P(('dp', 'expert')), may hold values from -0.09375 to 0.09375
- expert_down: bfloat16 [32, 768, 4096], P(('dp', 'expert')), may hold values from -0.21875 to 0.21875
- shared_gate: bfloat16 [4096, 4096], P(('dp', 'expert')), may hold values from -0.09375 to 0.09375
- shared_up: bfloat16 [4096, 4096], P(('dp', 'expert')), may hold values from -0.09375 to 0.09375
- shared_down: bfloat16 [4096, 4096], P(('dp', 'expert')), may hold values from -0.09375 to 0.09375
Outputs:
- block_out: bfloat16 [4096, 4096], P(('dp', 'expert'))
Inputs may be any that keep to these rules, and one draw needn't show every extreme that they name: `chosen`: token t lies in the rows of device t // 128 (devices numbered dp-major). Each expert's 128 indices are different; at most 8 of them lie in the rows of one device, and for every expert some device gives exactly 8.
All inputs are finite; a program needn't handle non-finite values.
Results may differ from a plain program's by a relative error of at most 0.0052.
Values may be sent and summed in bfloat16 or wider, within the bound.
A program may use at most 128 MiB of HBM per device.

v0:
```python
import jax
import jax.numpy as jnp
from jax import lax
from jax.sharding import PartitionSpec as P


def expert_rows(rows, w_gate, w_up, w_down):
    gated = jnp.dot(rows, w_gate, preferred_element_type=jnp.float32)
    lifted = jnp.dot(rows, w_up, preferred_element_type=jnp.float32)
    hidden = (jax.nn.silu(gated) * lifted).astype(jnp.bfloat16)
    return jnp.dot(hidden, w_down, preferred_element_type=jnp.float32).astype(jnp.bfloat16)


def slot_tables(levels, wanted, start_positions, slot_total, row_total):
    ranking = jnp.cumsum(wanted.astype(jnp.int32), axis=1) - 1
    slot_ids = jnp.arange(slot_total, dtype=jnp.int32)
    picks = wanted[:, :, None] & (ranking[:, :, None] == slot_ids[None, None, :])
    row_index = jnp.sum(jnp.where(picks, start_positions[:, :, None], 0), axis=1).reshape(-1)
    filled = jnp.any(picks, axis=1).reshape(-1)
    capacity_gating_weight = jnp.sum(jnp.where(picks, levels[:, :, None], 0.0), axis=1).reshape(-1)
    row_ids = jnp.arange(row_total, dtype=jnp.int32)
    member = (row_index[None, :] == row_ids[:, None]) & filled[None, :]
    selector = member.astype(jnp.bfloat16)
    weighted = jnp.where(member, capacity_gating_weight[None, :], 0.0).astype(jnp.bfloat16)
    return (selector, weighted)


def local(
    tokens,
    chosen,
    gate_levels,
    expert_gate,
    expert_up,
    expert_down,
    shared_gate,
    shared_up,
    shared_down,
):
    n_data = lax.axis_size("dp")
    n_expert = lax.axis_size("expert")
    accelerator_roster = n_data * n_expert
    tok_dev = tokens.shape[0]
    width = tokens.shape[1]
    slot_most = 2 * tok_dev // accelerator_roster
    row_data = lax.axis_index("dp")
    row_expert = lax.axis_index("expert")
    multiplier_factors = gate_levels.astype(jnp.float32) / 256.0
    pick_rows = (((0,), (0,)), ((), ()))
    contract = (((1,), (1,)), ((), ()))
    column = lax.all_gather(tokens, "dp", axis=0, tiled=True)
    gate_rows, up_rows, down_rows = (
        lax.all_gather(shared_gate, "expert", axis=0, tiled=True),
        lax.all_gather(shared_up, "expert", axis=0, tiled=True),
        lax.all_gather(shared_down, "expert", axis=0, tiled=True),
    )
    gated = lax.dot_general(column, gate_rows, contract, preferred_element_type=jnp.float32)
    lifted = lax.dot_general(column, up_rows, contract, preferred_element_type=jnp.float32)
    shared_hidden = (jax.nn.silu(gated) * lifted).astype(jnp.bfloat16)
    routed_own = None
    myself = row_data * n_expert + row_expert
    wanted = chosen // tok_dev == myself
    selector, weighted = slot_tables(
        multiplier_factors, wanted, chosen % tok_dev, slot_most, tok_dev
    )
    outgoing = lax.dot_general(selector, tokens, pick_rows, preferred_element_type=jnp.float32)
    outgoing, weighted = (outgoing.astype(jnp.bfloat16), weighted)
    outgoing = outgoing.reshape(accelerator_roster, slot_most, width)
    received = lax.all_to_all(outgoing, ("dp", "expert"), split_axis=0, concat_axis=0, tiled=True)
    flat = received.reshape(-1, width)
    returned = lax.all_to_all(
        expert_rows(flat, expert_gate[0], expert_up[0], expert_down[0]).reshape(received.shape),
        ("dp", "expert"),
        split_axis=0,
        concat_axis=0,
        tiled=True,
    )
    routed_own = jnp.dot(weighted, returned.reshape(-1, width), preferred_element_type=jnp.float32)
    value = jnp.dot(shared_hidden, down_rows, preferred_element_type=jnp.float32)
    combined = lax.psum_scatter(value, "dp", scatter_dimension=0, tiled=True)
    combined = combined + routed_own
    return combined.astype(jnp.bfloat16)


def solution(mesh):
    placed = (
        P(("dp", "expert"), None),
        P(),
        P(),
        P(("dp", "expert"), None, None),
        P(("dp", "expert"), None, None),
        P(("dp", "expert"), None, None),
        P(("dp", "expert"), None),
        P(("dp", "expert"), None),
        P(("dp", "expert"), None),
    )
    return jax.shard_map(
        local, mesh=mesh, in_specs=placed, out_specs=P(("dp", "expert"), None), check_vma=False
    )
```

profile of v0, /device:TPU:2, one launch (start us, length us, event | category | flops | bytes accessed | tf_op | source)
XLA Modules:
  0.0 514.4 jit_solution(7123957170573335426)
XLA Ops:
  6.5 0.7 all-gather.5.cloned.1.call-update
  7.3 0.7 all-gather.7.cloned.1.call-update
  8.1 0.7 all-gather.11.cloned.1.call-update
  8.8 0.5 all-gather.9.cloned.1.call-update
  9.4 81.6 %all-gather.5.cloned.1.call-done = bf16[512,4096]{1,0:T(8,128)(2,1)} async-done(((bf16[128,4096]{1,0:T(8,128)(2,1)}), bf16[512,4096]{1,0:T(8,128)(2,1)}) %all-gather.5.cloned.1.call-update) | async-done | bytes 4194320 | tf_op jit(solution)/shard_map/all_gather | solution.py:50
  91.0 54.8 %all-gather.7.cloned.1.call-done = bf16[1024,4096]{1,0:T(8,128)(2,1)} async-done(((bf16[128,4096]{1,0:T(8,128)(2,1)}), bf16[1024,4096]{1,0:T(8,128)(2,1)}) %all-gather.7.cloned.1.call-update) | async-done | bytes 8388624 | tf_op jit(solution)/shard_map/all_gather | solution.py:52
  145.8 8.2 %fusion.49 = f32[512,1024]{1,0:T(8,128)S(1)} fusion(bf16[512,4096]{1,0:T(8,128)(2,1)} %all-gather.5.cloned.1.call-done, bf16[1024,4096]{1,0:T(8,128)(2,1)} %all-gather.7.cloned.1.call-done), kind=kOutput, calls=%fused_computation.47 | convolution fusion | flops 4294967296 | bytes 14680064 | tf_op jit(solution)/shard_map/dot_general | solution.py:56
  154.0 48.1 %all-gather.11.cloned.1.call-done = bf16[1024,4096]{1,0:T(8,128)(2,1)} async-done(((bf16[128,4096]{1,0:T(8,128)(2,1)}), bf16[1024,4096]{1,0:T(8,128)(2,1)}) %all-gather.11.cloned.1.call-update) | async-done | bytes 8388624 | tf_op jit(solution)/shard_map/all_gather | solution.py:54
  202.1 56.2 %all-gather.9.cloned.1.call-done = bf16[1024,4096]{1,0:T(8,128)(2,1)} async-done(((bf16[128,4096]{1,0:T(8,128)(2,1)}), bf16[1024,4096]{1,0:T(8,128)(2,1)}) %all-gather.9.cloned.1.call-update) | async-done | bytes 8388624 | tf_op jit(solution)/shard_map/all_gather | solution.py:53
  258.3 19.1 %fusion.50 = f32[512,4096]{1,0:T(8,128)} fusion(bf16[1024,4096]{1,0:T(8,128)(2,1)} %all-gather.11.cloned.1.call-done, f32[512,1024]{1,0:T(8,128)S(1)} %fusion.49, bf16[512,4096]{1,0:T(8,128)(2,1)} %all-gather.5.cloned.1.call-done, bf16[1024,4096]{1,0:T(8,128)(2,1)} %all-gather.9.cloned.1.call-done), kind=kOutput, calls=%fused_computation.48 | convolution fusion | flops 8593080320 | bytes 31457280 | tf_op jit(solution)/shard_map/dot_general | solution.py:78
  277.4 0.7 copy-done.1
  278.1 0.3 reduce_window_sum.11
  278.4 0.6 select_reduce_fusion.1
  279.1 0.6 fusion.33
  279.8 0.1 and.34
  279.9 0.8 fusion.12
  280.7 107.9 %all_to_all.10 = bf16[32,8,4096]{2,1,0:T(8,128)(2,1)S(1)} all-to-all(bf16[32,8,4096]{2,1,0:T(8,128)(2,1)S(1)} %fusion.12), channel_id=1, replica_groups=mesh['dp'=4,'expert'=8] {'dp','expert'}, dimensions={0} | all-to-all | bytes 4194304 | tf_op jit(solution)/shard_map/all_to_all | solution.py:68
  388.6 4.6 fusion.4
  393.2 10.9 %fusion.9 = bf16[32,8,4096]{2,1,0:T(8,128)(2,1)} fusion(bf16[1,768,4096]{2,1,0:T(8,128)(2,1)} %param.14, bf16[1,4096,768]{2,1,0:T(8,128)(2,1)} %param.13, bf16[32,8,4096]{2,1,0:T(8,128)(2,1)S(1)} %all_to_all.10, f32[256,768]{1,0:T(8,128)S(1)} %fusion.4), kind=kOutput, calls=%fused_computation.8 | convolution fusion | flops 3223453696 | bytes 17563648 | tf_op jit(solution)/shard_map/dot_general | solution.py:11
  404.1 5.4 %all-to-all-start.1 = ((bf16[32,8,4096]{2,1,0:T(8,128)(2,1)}), bf16[32,8,4096]{2,1,0:T(8,128)(2,1)S(1)}, u32[]{:S(2)}, u32[]{:S(2)}) async-start(bf16[32,8,4096]{2,1,0:T(8,128)(2,1)} %fusion.9), calls=%async_computation.2 | async-start | bytes 4194304 | tf_op jit(solution)/shard_map/all_to_all | solution.py:70
  409.5 0.1 select_reduce_fusion
  409.7 91.6 %all-to-all-done.1 = bf16[32,8,4096]{2,1,0:T(8,128)(2,1)S(1)} async-done(((bf16[32,8,4096]{2,1,0:T(8,128)(2,1)}), bf16[32,8,4096]{2,1,0:T(8,128)(2,1)S(1)}, u32[]{:S(2)}, u32[]{:S(2)}) %all-to-all-start.1) | async-done | bytes 2097184 | tf_op jit(solution)/shard_map/all_to_all | solution.py:70
  501.4 3.5 reduce-scatter.2.cloned.1.call-done
  504.8 3.1 fusion.13
  (16 shorter events, 0.4 us)
Async XLA Ops:
  6.5 84.5 %all-gather.5.cloned.1.call-start = ((), (), s32[]{:S(2)}) async-start(), calls=%async_computation.3 | async-start | bytes 5242880 | tf_op jit(solution)/shard_map/all_gather | solution.py:50
  7.3 138.5 %all-gather.7.cloned.1.call-start = ((), (), s32[]{:S(2)}) async-start(), calls=%async_computation.4 | async-start | bytes 9437184 | tf_op jit(solution)/shard_map/all_gather | solution.py:52
  8.0 194.1 %all-gather.11.cloned.1.call-start = ((), (), s32[]{:S(2)}) async-start(), calls=%async_computation.6 | async-start | bytes 9437184 | tf_op jit(solution)/shard_map/all_gather | solution.py:54
  8.7 249.5 %all-gather.9.cloned.1.call-start = ((), (), s32[]{:S(2)}) async-start(), calls=%async_computation.5 | async-start | bytes 9437184 | tf_op jit(solution)/shard_map/all_gather | solution.py:53
  9.3 495.5 %reduce-scatter.2.cloned.1.call-start = ((), (), s32[]{:S(2)}) async-start(), calls=%async_computation.7 | async-start | bytes 10485760 | tf_op jit(solution)/shard_map/reduce_scatter | solution.py:79
  277.4 0.7 copy-start.1
  277.4 2.5 copy-start
  404.1 5.4 %copy-start.2 = (s32[32,128]{1,0:T(8,128)S(1)}, s32[32,128]{1,0:T(8,128)}, u32[]{:S(2)}) copy-start(s32[32,128]{1,0:T(8,128)} %param.11) | copy-start | bytes 49156
  404.1 97.3 %all-to-all-start.1 = ((bf16[32,8,4096]{2,1,0:T(8,128)(2,1)}), bf16[32,8,4096]{2,1,0:T(8,128)(2,1)S(1)}, u32[]{:S(2)}, u32[]{:S(2)}) async-start(bf16[32,8,4096]{2,1,0:T(8,128)(2,1)} %fusion.9), calls=%async_computation.2 | async-start | bytes 4194304 | tf_op jit(solution)/shard_map/all_to_all | solution.py:70
Sparse Core Ops, SparseCore 0:
  8.9 82.0 all-gather.4
  92.9 52.8 all-gather.6
  147.7 54.3 all-gather.10
  203.9 54.3 all-gather.8
  277.5 227.2 reduce-scatter.1
where the time goes:
time: 522 us; the launch traced here: 514 us
  waiting for transfers between devices  338 us (65%)
  blocking collectives  108 us (21%)
  matrix products  46.6 us (9%)
  between operations  13.2 us (3%)
  starting transfers between devices  5.55 us (1%)
    all_to_all x1, blocking collectives, local(): lax.all_to_all(outgoing, ('dp', 'expert'), split_axis=0, concat_axis=0, t...  108 us
    all_to_all x1, waiting for transfers between devices, local(): lax.all_to_all(expert_rows(flat, expert_gate[0], expert_up[0], expert_dow...  91.6 us
    all_gather x1, waiting for transfers between devices, local(): column = lax.all_gather(tokens, 'dp', axis=0, tiled=True)  81.6 us
    all_gather x1, waiting for transfers between devices, local(): lax.all_gather(shared_up, 'expert', axis=0, tiled=True)  56.2 us
    all_gather x1, waiting for transfers between devices, local(): lax.all_gather(shared_gate, 'expert', axis=0, tiled=True)  54.8 us
    all_gather x1, waiting for transfers between devices, local(): lax.all_gather(shared_down, 'expert', axis=0, tiled=True)  48.1 us
    dot_general x1, matrix products, local(): jnp.dot(shared_hidden, down_rows, preferred_element_type=jnp.float32)  19.1 us
    dot_general x1, matrix products, expert_rows(): jnp.dot(hidden, w_down, preferred_element_type=jnp.float32)  10.9 us
  transfers between devices with their start and end apart: 6, of which 6 were waited for; matrix products, arithmetic and copies ran while one was open for 5% of the time, Pallas kernels for 0%

commit v1 on v0

v1 whole, which is shorter than its diff:
```python
import functools

import jax
import jax.numpy as jnp
from jax import lax
from jax.experimental import pallas as pl
from jax.experimental.pallas import tpu as pltpu
from jax.sharding import PartitionSpec as P

MESH = pl.DeviceIdType.MESH
CHUNKS = 2
NT = (((1,), (1,)), ((), ()))


def flipped(index, mask, bits):
    out = 0
    for b in range(bits):
        bit = (index // (1 << b)) % 2
        if (mask >> b) & 1:
            bit = 1 - bit
        out = out + bit * (1 << b)
    return out


def block_kernel(
    n_dp, n_e, slots,
    tokens, sh_gate, sh_up, sh_down, ex_gate, ex_up, ex_down, sel, wsel,
    out,
    tok, wg, wu, wd, xg, xu, xd, sbuf, rbuf, ret, hidden, xhid, rs, own,
    local_sem, tok_send, tok_recv,
    dsend, drecv, ssend, srecv,
    a_send, a_recv, r_send, r_recv, z_send, z_recv,
):
    d = lax.axis_index("dp")
    e = lax.axis_index("expert")
    rows, width = tokens.shape
    hs = sh_gate.shape[0]
    ffr = ex_gate.shape[1]
    col = width // CHUNKS
    bits = n_e.bit_length() - 1
    pairs = n_e // 2
    relay = pairs == 4
    half = hs // 2
    group = n_dp * slots

    def dev_e(mask):
        return (d, flipped(e, mask, bits))

    def dev_d(step):
        return ((d + step) % n_dp, e)

    barrier = pltpu.get_barrier_semaphore()
    for j in range(1, n_e):
        pl.semaphore_signal(barrier, inc=1, device_id=dev_e(j), device_id_type=MESH)
    for j in range(1, n_dp):
        pl.semaphore_signal(barrier, inc=1, device_id=dev_d(j), device_id_type=MESH)
    pl.semaphore_wait(barrier, n_e - 1 + n_dp - 1)

    def remote(src, dst, s, r, dev):
        return pltpu.make_async_remote_copy(
            src_ref=src, dst_ref=dst, send_sem=s, recv_sem=r, device_id=dev, device_id_type=MESH
        )

    units = [(sh_gate, wg, 0, width), (sh_up, wu, 0, width)]
    units += [(sh_down, wd, c * col, col) for c in range(CHUNKS)]

    def mine(u):
        src, _, c0, cn = units[u]
        return src.at[:, pl.ds(c0, cn)]

    def spot(u, mask, r0=0, rn=None):
        _, buf, c0, cn = units[u]
        start = pl.multiple_of(flipped(e, mask, bits) * hs + r0, 16)
        return buf.at[pl.ds(start, hs if rn is None else rn), pl.ds(c0, cn)]

    def local(u):
        return pltpu.make_async_copy(mine(u), spot(u, 0), local_sem.at[u])

    def direct(u, k):
        return remote(mine(u), spot(u, 0), dsend.at[u, k], drecv.at[u, k], dev_e(2 * k))

    def direct_in(u, k):
        return remote(spot(u, 2 * k), spot(u, 2 * k), dsend.at[u, k], drecv.at[u, k], dev_e(2 * k))

    def onward(u, i):
        part = spot(u, 2 * (i + 1), i * half, half)
        return remote(part, part, dsend.at[u, 3 + i], drecv.at[u, 3 + i], dev_e(2 * (2 - i)))

    def onward_in(u, i):
        part = spot(u, 6, i * half, half)
        return remote(part, part, dsend.at[u, 3 + i], drecv.at[u, 3 + i], dev_e(2 * (2 - i)))

    def sibling(u, k):
        src = mine(u) if k == 0 else spot(u, 2 * k)
        return remote(src, spot(u, 2 * k), ssend.at[u, k], srecv.at[u, k], dev_e(1))

    def sibling_in(u, k):
        part = spot(u, 2 * k + 1)
        return remote(part, part, ssend.at[u, k], srecv.at[u, k], dev_e(1))

    near = (1, 2) if relay else tuple(range(1, pairs))

    def begin(u):
        for k in near:
            direct(u, k).start()
        sibling(u, 0).start()
        local(u).start()

    def spread(u):
        for k in near:
            direct_in(u, k).wait_recv()
            if relay:
                onward(u, k - 1).start()
            sibling(u, k).start()

    def finish(u):
        if relay:
            onward_in(u, 0).wait_recv()
            onward_in(u, 1).wait_recv()
            sibling(u, 3).start()

    def complete(u):
        local(u).wait()
        for k in range(pairs):
            sibling_in(u, k).wait_recv()

    def drain(u):
        for k in near:
            direct(u, k).wait_send()
        if relay:
            onward(u, 0).wait_send()
            onward(u, 1).wait_send()
        for k in range(pairs):
            sibling(u, k).wait_send()

    def tok_spot(step):
        start = pl.multiple_of(((d + step) % n_dp) * rows, 16)
        return tok.at[pl.ds(start, rows)]

    def tok_out(j):
        return remote(tokens, tok_spot(0), tok_send.at[j], tok_recv.at[j], dev_d(j))

    def tok_in(j):
        return remote(tok_spot(n_dp - j), tok_spot(n_dp - j), tok_send.at[j], tok_recv.at[j], dev_d(j))

    tok_own = pltpu.make_async_copy(tokens, tok_spot(0), local_sem.at[2 + CHUNKS])
    for j in range(1, n_dp):
        tok_out(j).start()
    tok_own.start()
    begin(0)
    begin(1)
    stage = [
        pltpu.make_async_copy(src, dst, local_sem.at[3 + CHUNKS + i])
        for i, (src, dst) in enumerate(((ex_gate, xg), (ex_up, xu), (ex_down, xd)))
    ]
    for copy in stage:
        copy.start()

    spread(0)
    begin(2)
    spread(1)
    finish(0)
    finish(1)

    for j in range(1, n_dp):
        tok_in(j).wait_recv()
    tok_own.wait()

    step_cols = 512

    @pl.loop(0, width // step_cols)
    def _(i):
        c = pl.ds(pl.multiple_of(i * step_cols, step_cols), step_cols)
        sbuf[:, c] = jnp.dot(sel[...], tok[:, c], preferred_element_type=jnp.float32).astype(jnp.bfloat16)

    def group_rows(mask):
        return pl.ds(pl.multiple_of(flipped(e, mask, bits) * group, 16), group)

    def a_out(j):
        return remote(sbuf.at[group_rows(j)], rbuf.at[group_rows(0)], a_send.at[j], a_recv.at[j], dev_e(j))

    def a_in(j):
        return remote(sbuf.at[group_rows(j)], rbuf.at[group_rows(j)], a_send.at[j], a_recv.at[j], dev_e(j))

    a_own = pltpu.make_async_copy(sbuf.at[group_rows(0)], rbuf.at[group_rows(0)], a_send.at[0])
    for j in range(n_e - 1, 0, -1):
        a_out(j).start()
    a_own.start()

    for c in range(1, CHUNKS):
        begin(2 + c)
    spread(2)
    complete(0)
    complete(1)

    block = 256

    @pl.loop(0, n_e * hs // block)
    def _(i):
        r = pl.ds(pl.multiple_of(i * block, block), block)
        g = lax.dot_general(tok[...], wg[r, :], NT, preferred_element_type=jnp.float32)
        v = lax.dot_general(tok[...], wu[r, :], NT, preferred_element_type=jnp.float32)
        hidden[:, r] = (g / (1.0 + jnp.exp(-g)) * v).astype(jnp.bfloat16)

    finish(2)

    for copy in stage:
        copy.wait()
    for j in range(1, n_e):
        a_in(j).wait_recv()
    a_own.wait()

    @pl.loop(0, ffr // 256)
    def _(i):
        f = pl.ds(pl.multiple_of(i * 256, 256), 256)
        g = jnp.dot(rbuf[...], xg[:, f], preferred_element_type=jnp.float32)
        v = jnp.dot(rbuf[...], xu[:, f], preferred_element_type=jnp.float32)
        xhid[:, f] = (g / (1.0 + jnp.exp(-g)) * v).astype(jnp.bfloat16)

    for j in range(1, n_e):
        a_out(j).wait_send()

    def r_out(c, j):
        cc = pl.ds(c * col, col)
        return remote(
            sbuf.at[group_rows(j), cc], ret.at[group_rows(0), cc], r_send.at[c, j], r_recv.at[c, j], dev_e(j)
        )

    def r_in(c, j):
        cc = pl.ds(c * col, col)
        return remote(
            sbuf.at[group_rows(j), cc], ret.at[group_rows(j), cc], r_send.at[c, j], r_recv.at[c, j], dev_e(j)
        )

    def r_own(c):
        cc = pl.ds(c * col, col)
        return pltpu.make_async_copy(sbuf.at[group_rows(0), cc], ret.at[group_rows(0), cc], r_send.at[c, 0])

    for c in range(CHUNKS):
        @pl.loop(0, col // step_cols)
        def _(i):
            cc = pl.ds(pl.multiple_of(c * col + i * step_cols, step_cols), step_cols)
            sbuf[:, cc] = jnp.dot(xhid[...], xd[:, cc], preferred_element_type=jnp.float32).astype(jnp.bfloat16)

        for j in range(n_e - 1, 0, -1):
            r_out(c, j).start()
        r_own(c).start()

    def z_out(c, j):
        start = pl.multiple_of(((d + j) % n_dp) * rows, 16)
        cc = pl.ds(c * col, col)
        return remote(
            tok.at[pl.ds(start, rows), cc], rs.at[pl.ds((j - 1) * rows, rows), cc],
            z_send.at[c, j], z_recv.at[c, j], dev_d(j),
        )

    def partial(target, cc):
        r = pl.ds(pl.multiple_of(target * rows, 16), rows)
        return jnp.dot(hidden[r, :], wd[:, cc], preferred_element_type=jnp.float32) + jnp.dot(
            wsel[r, :], ret[:, cc], preferred_element_type=jnp.float32
        )

    for c in range(CHUNKS):
        if c > 0:
            spread(2 + c)
            finish(2 + c)
        complete(2 + c)
        for j in range(1, n_e):
            r_in(c, j).wait_recv()
        r_own(c).wait()
        for j in range(n_dp - 1, -1, -1):
            target = (d + j) % n_dp

            @pl.loop(0, col // step_cols)
            def _(i):
                cc = pl.ds(pl.multiple_of(c * col + i * step_cols, step_cols), step_cols)
                value = partial(target, cc)
                if j == 0:
                    own[:, cc] = value
                else:
                    r = pl.ds(pl.multiple_of(target * rows, 16), rows)
                    tok[r, cc] = value.astype(jnp.bfloat16)

            if j > 0:
                z_out(c, j).start()

    for c in range(CHUNKS):
        for j in range(1, n_dp):
            z_out(c, j).wait_recv()

        @pl.loop(0, col // step_cols)
        def _(i):
            cc = pl.ds(pl.multiple_of(c * col + i * step_cols, step_cols), step_cols)
            total = own[:, cc]
            for j in range(1, n_dp):
                total = total + rs[pl.ds((j - 1) * rows, rows), cc].astype(jnp.float32)
            out[:, cc] = total.astype(jnp.bfloat16)

    for u in range(2 + CHUNKS):
        drain(u)
    for j in range(1, n_dp):
        tok_out(j).wait_send()
    for c in range(CHUNKS):
        for j in range(1, n_e):
            r_out(c, j).wait_send()
        for j in range(1, n_dp):
            z_out(c, j).wait_send()


def slot_tables(chosen, levels, n_dp, n_e, tok_dev, slots):
    d = lax.axis_index("dp")
    e = lax.axis_index("expert")
    picked = lax.dynamic_slice_in_dim(chosen, d * n_e, n_e, 0)
    scale = lax.dynamic_slice_in_dim(levels, d * n_e, n_e, 0).astype(jnp.float32) / 256.0
    holders = jnp.arange(n_dp, dtype=jnp.int32) * n_e + e
    wanted = picked[:, None, :] // tok_dev == holders[None, :, None]
    rank = jnp.cumsum(wanted.astype(jnp.int32), axis=2) - 1
    slot_ids = jnp.arange(slots, dtype=jnp.int32)
    picks = wanted[:, :, None, :] & (rank[:, :, None, :] == slot_ids[None, None, :, None])
    position = (picked % tok_dev)[:, None, None, :]
    row = jnp.sum(jnp.where(picks, position, 0), axis=3)
    row = (row + jnp.arange(n_dp, dtype=jnp.int32)[None, :, None] * tok_dev).reshape(-1)
    filled = jnp.any(picks, axis=3).reshape(-1)
    weight = jnp.sum(jnp.where(picks, scale[:, None, None, :], 0.0), axis=3).reshape(-1)
    ids = jnp.arange(n_dp * tok_dev, dtype=jnp.int32)
    sel = ((row[:, None] == ids[None, :]) & filled[:, None]).astype(jnp.bfloat16)
    member = (row[None, :] == ids[:, None]) & filled[None, :]
    wsel = jnp.where(member, weight[None, :], 0.0).astype(jnp.bfloat16)
    return sel, wsel


def local(
    tokens, chosen, gate_levels, expert_gate, expert_up, expert_down, shared_gate, shared_up, shared_down,
    *, n_dp, n_e,
):
    rows, width = tokens.shape
    hs = shared_gate.shape[0]
    ffr = expert_gate.shape[2]
    slots = 2 * rows // (n_dp * n_e)
    sel, wsel = slot_tables(chosen, gate_levels, n_dp, n_e, rows, slots)
    taken = n_e * n_dp * slots
    pairs = n_e // 2
    units = 2 + CHUNKS
    dma = pltpu.SemaphoreType.DMA
    bf16 = jnp.bfloat16
    any_spec = pl.BlockSpec(memory_space=pl.ANY)
    vmem_spec = pl.BlockSpec(memory_space=pltpu.VMEM)
    return pl.pallas_call(
        functools.partial(block_kernel, n_dp, n_e, slots),
        out_shape=jax.ShapeDtypeStruct((rows, width), bf16),
        in_specs=[any_spec] * 7 + [vmem_spec] * 2,
        out_specs=vmem_spec,
        scratch_shapes=[
            pltpu.VMEM((n_dp * rows, width), bf16),
            pltpu.VMEM((n_e * hs, width), bf16),
            pltpu.VMEM((n_e * hs, width), bf16),
            pltpu.VMEM((n_e * hs, width), bf16),
            pltpu.VMEM((width, ffr), bf16),
            pltpu.VMEM((width, ffr), bf16),
            pltpu.VMEM((ffr, width), bf16),
            pltpu.VMEM((taken, width), bf16),
            pltpu.VMEM((taken, width), bf16),
            pltpu.VMEM((taken, width), bf16),
            pltpu.VMEM((n_dp * rows, n_e * hs), bf16),
            pltpu.VMEM((taken, ffr), bf16),
            pltpu.VMEM(((n_dp - 1) * rows, width), bf16),
            pltpu.VMEM((rows, width), jnp.float32),
            dma((6 + CHUNKS,)),
            dma((n_dp,)),
            dma((n_dp,)),
            dma((units, max(pairs, 5))),
            dma((units, max(pairs, 5))),
            dma((units, pairs)),
            dma((units, pairs)),
            dma((n_e,)),
            dma((n_e,)),
            dma((CHUNKS, n_e)),
            dma((CHUNKS, n_e)),
            dma((CHUNKS, n_dp)),
            dma((CHUNKS, n_dp)),
        ],
        compiler_params=pltpu.CompilerParams(
            collective_id=0, has_side_effects=True, vmem_limit_bytes=63 * 2**20
        ),
    )(
        tokens, shared_gate, shared_up, shared_down,
        expert_gate[0], expert_up[0], expert_down[0], sel, wsel,
    )


def solution(mesh):
    both = ("dp", "expert")
    two = P(both, None)
    three = P(both, None, None)
    return jax.shard_map(
        functools.partial(local, n_dp=mesh.shape["dp"], n_e=mesh.shape["expert"]),
        mesh=mesh,
        in_specs=(two, P(), P(), three, three, three, two, two, two),
        out_specs=two,
        check_vma=False,
    )
```

time: 522 us -> 253 us (0.48); the launches traced: 514 us -> 253 us
  waiting for transfers between devices: 338 us -> 0 us
  Pallas kernels: 0 us -> 244 us
  blocking collectives: 108 us -> 0 us
  matrix products: 46.6 us -> 0 us
  between operations: 13.2 us -> 0.03 us
  starting transfers between devices: 5.55 us -> 0 us
    pallas_call x0 -> x1, Pallas kernels: none -> 244 us  [local(): pl.pallas_call(functools.partial(block_kernel, n_dp, n_e, slots), out_sha...]
    all_gather x4 -> x0, waiting for transfers between devices: 241 us -> none  [the longest x1 81.6 us: local(): column = lax.all_gather(tokens, 'dp', axis=0, tiled=True)]
    all_to_all x1 -> x0, blocking collectives: 108 us -> none  [local(): lax.all_to_all(outgoing, ('dp', 'expert'), split_axis=0, concat_axis=0, t...]
    all_to_all x1 -> x0, waiting for transfers between devices: 91.6 us -> none  [local(): lax.all_to_all(expert_rows(flat, expert_gate[0], expert_up[0], expert_dow...]
    dot_general x6 -> x0, matrix products: 46.6 us -> none  [the longest x1 19.1 us: local(): jnp.dot(shared_hidden, down_rows, preferred_element_type=jnp.float32)]
    all_to_all x1 -> x0, starting transfers between devices: 5.4 us -> none  [local(): lax.all_to_all(expert_rows(flat, expert_gate[0], expert_up[0], expert_dow...]
  transfers between devices with their start and end apart: 6 -> 0, of which waited for: 6 -> 0; matrix products, arithmetic and copies ran while one was open for 5% -> 0% of each run, Pallas kernels for 0% -> 0%
where the time goes in v1:
time: 253 us
  Pallas kernels  244 us (96%)
  other arithmetic  6.5 us (3%)
  local copies, waits for them, and re-layouts  2.6 us (1%)
    pallas_call x1, Pallas kernels, local(): pl.pallas_call(functools.partial(block_kernel, n_dp, n_e, slots), out_sha...  244 us

profile of v1, /device:TPU:2, one launch (start us, length us, event | category | flops | bytes accessed | tf_op | source)
XLA Modules:
  0.0 253.0 jit_solution(11475126489072727218)
XLA Ops:
  0.0 0.7 convert_multiply_fusion
  0.7 0.7 add_select_fusion.1
  1.4 0.7 add_select_fusion
  2.1 0.1 fusion.7
  2.2 1.1 reduce_window_sum.11
  3.3 0.1 select_reduce_fusion
  3.5 0.1 broadcast_in_dim.52
  3.6 0.6 fusion.4
  4.2 0.6 select_reduce_fusion.1
  4.8 0.1 and.44
  4.9 0.1 broadcast_add_fusion
  5.0 0.1 add.52
  5.1 0.9 select_convert_fusion.wsel
  6.0 0.9 fusion.1.sel
  6.8 243.9 %shard_map.91 = bf16[128,4096]{1,0:T(8,128)(2,1)} custom-call(bf16[128,4096]{1,0:T(8,128)(2,1)} %tokens.1, bf16[128,4096]{1,0:T(8,128)(2,1)} %sh_gate.1, bf16[128,4096]{1,0:T(8,128)(2,1)} %sh_up.1, bf16[128,4096]{1,0:T(8,128)(2,1)} %sh_down.1, bf16[4096,768]{1,0:T(8,128)(2,1)} %bitcast.3, bf16[4096,768]{1,0:T(8,128)(2,1)} %bitcast.4, ...), custom_call_target="tpu_custom_call" | custom-call | tf_op jit(solution)/shard_map/pallas_call | solution.py:348
  250.7 2.3 copy.15
  (5 shorter events, 0.0 us)

commit v2 on v1

--- a/solution.py
+++ b/solution.py
@@ -8,7 +8,8 @@
 from jax.sharding import PartitionSpec as P
 
 MESH = pl.DeviceIdType.MESH
-CHUNKS = 2
+CHUNKS = 4
+EARLY = 2
 NT = (((1,), (1,)), ((), ()))
 
 
@@ -46,14 +47,14 @@
     def dev_e(mask):
         return (d, flipped(e, mask, bits))
 
-    def dev_d(step):
-        return ((d + step) % n_dp, e)
-
     barrier = pltpu.get_barrier_semaphore()
     for j in range(1, n_e):
         pl.semaphore_signal(barrier, inc=1, device_id=dev_e(j), device_id_type=MESH)
+    left, right = (d - 1, e), (d + 1, e)
+    has_left, has_right = d > 0, d < n_dp - 1
+
     for j in range(1, n_dp):
-        pl.semaphore_signal(barrier, inc=1, device_id=dev_d(j), device_id_type=MESH)
+        pl.semaphore_signal(barrier, inc=1, device_id=((d + j) % n_dp, e), device_id_type=MESH)
     pl.semaphore_wait(barrier, n_e - 1 + n_dp - 1)
 
     def remote(src, dst, s, r, dev):
@@ -133,19 +134,51 @@
         for k in range(pairs):
             sibling(u, k).wait_send()
 
-    def tok_spot(step):
-        start = pl.multiple_of(((d + step) % n_dp) * rows, 16)
-        return tok.at[pl.ds(start, rows)]
-
-    def tok_out(j):
-        return remote(tokens, tok_spot(0), tok_send.at[j], tok_recv.at[j], dev_d(j))
-
-    def tok_in(j):
-        return remote(tok_spot(n_dp - j), tok_spot(n_dp - j), tok_send.at[j], tok_recv.at[j], dev_d(j))
-
-    tok_own = pltpu.make_async_copy(tokens, tok_spot(0), local_sem.at[2 + CHUNKS])
-    for j in range(1, n_dp):
-        tok_out(j).start()
+    def tok_spot(index):
+        return tok.at[pl.ds(pl.multiple_of(index * rows, 16), rows)]
+
+    def tok_copy(h, way, src_index):
+        src = tokens if h == 1 else tok_spot(src_index)
+        return remote(
+            src, tok_spot(src_index), tok_send.at[way, h], tok_recv.at[way, h], right if way == 0 else left
+        )
+
+    def tok_start(h):
+        @pl.when((d - h + 1 >= 0) & has_right)
+        def _():
+            tok_copy(h, 0, d - h + 1).start()
+
+        @pl.when((d + h - 1 < n_dp) & has_left)
+        def _():
+            tok_copy(h, 1, d + h - 1).start()
+
+    def tok_wait(h):
+        @pl.when(d - h >= 0)
+        def _():
+            part = tok_spot(d - h)
+            remote(part, part, tok_send.at[0, h], tok_recv.at[0, h], left).wait_recv()
+
+        @pl.when(d + h < n_dp)
+        def _():
+            part = tok_spot(d + h)
+            remote(part, part, tok_send.at[1, h], tok_recv.at[1, h], right).wait_recv()
+
+    def tok_step(h):
+        tok_wait(h)
+        if h < n_dp - 1:
+            tok_start(h + 1)
+
+    def tok_drain(h):
+        @pl.when((d - h + 1 >= 0) & has_right)
+        def _():
+            tok_copy(h, 0, d - h + 1).wait_send()
+
+        @pl.when((d + h - 1 < n_dp) & has_left)
+        def _():
+            tok_copy(h, 1, d + h - 1).wait_send()
+
+    tok_own = pltpu.make_async_copy(tokens, tok_spot(d), local_sem.at[2 + CHUNKS])
+    tok_start(1)
     tok_own.start()
     begin(0)
     begin(1)
@@ -156,14 +189,17 @@
     for copy in stage:
         copy.start()
 
+    tok_step(1)
     spread(0)
-    begin(2)
+    for h in range(2, n_dp - 1):
+        tok_step(h)
     spread(1)
+    for c in range(EARLY):
+        begin(2 + c)
     finish(0)
     finish(1)
 
-    for j in range(1, n_dp):
-        tok_in(j).wait_recv()
+    tok_step(n_dp - 1)
     tok_own.wait()
 
     step_cols = 512
@@ -187,9 +223,8 @@
         a_out(j).start()
     a_own.start()
 
-    for c in range(1, CHUNKS):
-        begin(2 + c)
-    spread(2)
+    for c in range(EARLY):
+        spread(2 + c)
     complete(0)
     complete(1)
 
@@ -202,13 +237,18 @@
         v = lax.dot_general(tok[...], wu[r, :], NT, preferred_element_type=jnp.float32)
         hidden[:, r] = (g / (1.0 + jnp.exp(-g)) * v).astype(jnp.bfloat16)
 
-    finish(2)
+    for c in range(EARLY):
+        finish(2 + c)
+    for h in range(1, n_dp):
+        tok_drain(h)
 
     for copy in stage:
         copy.wait()
     for j in range(1, n_e):
         a_in(j).wait_recv()
     a_own.wait()
+    for c in range(EARLY, CHUNKS):
+        begin(2 + c)
 
     @pl.loop(0, ffr // 256)
     def _(i):
@@ -246,12 +286,26 @@
             r_out(c, j).start()
         r_own(c).start()
 
-    def z_out(c, j):
-        start = pl.multiple_of(((d + j) % n_dp) * rows, 16)
+    for c in range(EARLY, CHUNKS):
+        spread(2 + c)
+
+    def slot(t, way):
+        return pl.multiple_of((t + 1 - way) * rows, 16)
+
+    def z_copy(c, s, way):
+        t = d + s if way == 0 else d - s
         cc = pl.ds(c * col, col)
         return remote(
-            tok.at[pl.ds(start, rows), cc], rs.at[pl.ds((j - 1) * rows, rows), cc],
-            z_send.at[c, j], z_recv.at[c, j], dev_d(j),
+            tok.at[pl.ds(pl.multiple_of(t * rows, 16), rows), cc],
+            rs.at[pl.ds(slot(t, way), rows), cc],
+            z_send.at[c, way, s], z_recv.at[c, way, s - 1], right if way == 0 else left,
+        )
+
+    def z_in(c, s, way):
+        t = d + s if way == 0 else d - s
+        part = rs.at[pl.ds(slot(t, way), rows), pl.ds(c * col, col)]
+        return remote(
+            part, part, z_send.at[c, way, s], z_recv.at[c, way, s], left if way == 0 else right
         )
 
     def partial(target, cc):
@@ -260,51 +314,77 @@
             wsel[r, :], ret[:, cc], preferred_element_type=jnp.float32
         )
 
+    def pass_on(c, s, way):
+        t = d + s if way == 0 else d - s
+        r = pl.ds(pl.multiple_of(t * rows, 16), rows)
+        behind = has_left if way == 0 else has_right
+
+        @pl.when(behind)
+        def _():
+            z_in(c, s, way).wait_recv()
+
+            @pl.loop(0, col // step_cols)
+            def _(i):
+                cc = pl.ds(pl.multiple_of(c * col + i * step_cols, step_cols), step_cols)
+                value = partial(t, cc) + rs[pl.ds(slot(t, way), rows), cc].astype(jnp.float32)
+                tok[r, cc] = value.astype(jnp.bfloat16)
+
+        @pl.when(jnp.logical_not(behind))
+        def _():
+            @pl.loop(0, col // step_cols)
+            def _(i):
+                cc = pl.ds(pl.multiple_of(c * col + i * step_cols, step_cols), step_cols)
+                tok[r, cc] = partial(t, cc).astype(jnp.bfloat16)
+
+        z_copy(c, s, way).start()
+
     for c in range(CHUNKS):
-        if c > 0:
-            spread(2 + c)
-            finish(2 + c)
+        if c == EARLY - 1:
+            for later in range(EARLY, CHUNKS):
+                finish(2 + later)
         complete(2 + c)
         for j in range(1, n_e):
             r_in(c, j).wait_recv()
         r_own(c).wait()
-        for j in range(n_dp - 1, -1, -1):
-            target = (d + j) % n_dp
-
-            @pl.loop(0, col // step_cols)
-            def _(i):
-                cc = pl.ds(pl.multiple_of(c * col + i * step_cols, step_cols), step_cols)
-                value = partial(target, cc)
-                if j == 0:
-                    own[:, cc] = value
-                else:
-                    r = pl.ds(pl.multiple_of(target * rows, 16), rows)
-                    tok[r, cc] = value.astype(jnp.bfloat16)
-
-            if j > 0:
-                z_out(c, j).start()
-
-    for c in range(CHUNKS):
-        for j in range(1, n_dp):
-            z_out(c, j).wait_recv()
+        for s in range(n_dp - 1, 0, -1):
+            pl.when(d + s < n_dp)(functools.partial(pass_on, c, s, 0))
+            pl.when(d - s >= 0)(functools.partial(pass_on, c, s, 1))
 
         @pl.loop(0, col // step_cols)
         def _(i):
             cc = pl.ds(pl.multiple_of(c * col + i * step_cols, step_cols), step_cols)
-            total = own[:, cc]
-            for j in range(1, n_dp):
-                total = total + rs[pl.ds((j - 1) * rows, rows), cc].astype(jnp.float32)
-            out[:, cc] = total.astype(jnp.bfloat16)
+            own[:, cc] = partial(d, cc)
+
+    def add_in(c, way):
+        z_in(c, 0, way).wait_recv()
+
+        @pl.loop(0, col // step_cols)
+        def _(i):
+            cc = pl.ds(pl.multiple_of(c * col + i * step_cols, step_cols), step_cols)
+            own[:, cc] = own[:, cc] + rs[pl.ds(slot(d, way), rows), cc].astype(jnp.float32)
+
+    for c in range(CHUNKS):
+        pl.when(has_left)(functools.partial(add_in, c, 0))
+        pl.when(has_right)(functools.partial(add_in, c, 1))
+
+        @pl.loop(0, col // step_cols)
+        def _(i):
+            cc = pl.ds(pl.multiple_of(c * col + i * step_cols, step_cols), step_cols)
+            out[:, cc] = own[:, cc].astype(jnp.bfloat16)
 
     for u in range(2 + CHUNKS):
         drain(u)
-    for j in range(1, n_dp):
-        tok_out(j).wait_send()
     for c in range(CHUNKS):
         for j in range(1, n_e):
             r_out(c, j).wait_send()
-        for j in range(1, n_dp):
-            z_out(c, j).wait_send()
+        for s in range(1, n_dp):
+            @pl.when(d + s < n_dp)
+            def _():
+                z_copy(c, s, 0).wait_send()
+
+            @pl.when(d - s >= 0)
+            def _():
+                z_copy(c, s, 1).wait_send()
 
 
 def slot_tables(chosen, levels, n_dp, n_e, tok_dev, slots):
@@ -363,11 +443,11 @@
             pltpu.VMEM((taken, width), bf16),
             pltpu.VMEM((n_dp * rows, n_e * hs), bf16),
             pltpu.VMEM((taken, ffr), bf16),
-            pltpu.VMEM(((n_dp - 1) * rows, width), bf16),
+            pltpu.VMEM(((n_dp + 1) * rows, width), bf16),
             pltpu.VMEM((rows, width), jnp.float32),
             dma((6 + CHUNKS,)),
-            dma((n_dp,)),
-            dma((n_dp,)),
+            dma((2, n_dp)),
+            dma((2, n_dp)),
             dma((units, max(pairs, 5))),
             dma((units, max(pairs, 5))),
             dma((units, pairs)),
@@ -376,11 +456,11 @@
             dma((n_e,)),
             dma((CHUNKS, n_e)),
             dma((CHUNKS, n_e)),
-            dma((CHUNKS, n_dp)),
-            dma((CHUNKS, n_dp)),
+            dma((CHUNKS, 2, n_dp)),
+            dma((CHUNKS, 2, n_dp)),
         ],
         compiler_params=pltpu.CompilerParams(
-            collective_id=0, has_side_effects=True, vmem_limit_bytes=63 * 2**20
+            collective_id=0, has_side_effects=True, vmem_limit_bytes=64 * 2**20 - 2**18
         ),
     )(
         tokens, shared_gate, shared_up, shared_down,

time: 253 us -> 226 us (0.89); the launches traced: 253 us -> 223 us
  Pallas kernels: 244 us -> 214 us
    pallas_call x1, Pallas kernels: 244 us -> 214 us  [local(): pl.pallas_call(functools.partial(block_kernel, n_dp, n_e, slots), out_sha...]
where the time goes in v2:
time: 226 us; the launch traced here: 223 us
  Pallas kernels  214 us (95%)
  other arithmetic  6.5 us (3%)
  local copies, waits for them, and re-layouts  2.6 us (1%)
    pallas_call x1, Pallas kernels, local(): pl.pallas_call(functools.partial(block_kernel, n_dp, n_e, slots), out_sha...  214 us

profile of v2, /device:TPU:2, one launch (start us, length us, event | category | flops | bytes accessed | tf_op | source)
XLA Modules:
  0.0 223.1 jit_solution(15273291620976946240)
XLA Ops:
  0.0 0.7 convert_multiply_fusion
  0.7 0.7 add_select_fusion.1
  1.4 0.7 add_select_fusion
  2.1 0.1 fusion.7
  2.2 1.1 reduce_window_sum.11
  3.3 0.1 select_reduce_fusion
  3.5 0.1 broadcast_in_dim.52
  3.6 0.6 fusion.4
  4.2 0.6 select_reduce_fusion.1
  4.8 0.1 and.44
  4.9 0.1 broadcast_add_fusion
  5.0 0.1 add.52
  5.1 0.9 select_convert_fusion.wsel
  6.0 0.9 fusion.1.sel
  6.8 213.9 %shard_map.91 = bf16[128,4096]{1,0:T(8,128)(2,1)} custom-call(bf16[128,4096]{1,0:T(8,128)(2,1)} %tokens.1, bf16[128,4096]{1,0:T(8,128)(2,1)} %sh_gate.1, bf16[128,4096]{1,0:T(8,128)(2,1)} %sh_up.1, bf16[128,4096]{1,0:T(8,128)(2,1)} %sh_down.1, bf16[4096,768]{1,0:T(8,128)(2,1)} %bitcast.3, bf16[4096,768]{1,0:T(8,128)(2,1)} %bitcast.4, ...), custom_call_target="tpu_custom_call" | custom-call | tf_op jit(solution)/shard_map/pallas_call | solution.py:428
  220.8 2.3 %copy.15 = bf16[128,4096]{1,0:T(8,128)(2,1)} copy(bf16[128,4096]{1,0:T(8,128)(2,1)} %shard_map.91) | data formatting | bytes 2097152
  (5 shorter events, 0.0 us)
